TPU v7x, 256 devices: a whole 4x4x8 slice. The times are simulated.
256 devices in a mesh: gx: 8 (over z_hi, core), gy: 8 (over y, z_lo), gz: 4 (over x).
Axes of the slice: x: 4, y: 4, z: 8 (z_hi: 4, z_lo: 2; z = z_hi * 2 + z_lo), core: 2. Of those that a mesh axis runs over, the one named last changes fastest.
Arguments:
- pressure_prev: float32 [128, 192, 1024], P('gx', 'gy', 'gz'), may hold values from -6 to 6
- pressure_now: float32 [128, 192, 1024], P('gx', 'gy', 'gz'), may hold values from -6 to 6
- material: int32 [128, 192, 1024], P('gx', 'gy', 'gz'), may hold values from 0 to 7
- speed_table: float32 [8], replicated, may hold values from 0.05 to 0.32
- anchors: int32 [8, 8, 512], P('gx', 'gy', 'gz'), may hold values from 0 to 53496, as said below
- counts: int32 [8, 8, 4], P('gx', 'gy', 'gz'), may hold values from 64 to 128, as said below
- w_in: bfloat16 [512, 1024], replicated, may hold values from -0.25 to 0.25
- w_out: bfloat16 [1024, 512], replicated, may hold values from -0.1875 to 0.1875
Outputs:
- final_pressure: float32 [128, 192, 1024], P('gx', 'gy', 'gz')
- grad_in: float32 [512, 1024], P('gx')
- grad_out: float32 [1024, 512], P('gx')
Inputs may be any that keep to these rules, and one draw needn't show every extreme that they name: `anchors`: each entry is i * 24 * 256 + j * 256 + k with i <= 8, j <= 16, k <= 248, so every patch lies inside its brick; entries of a brick may repeat. The used slots of a brick are its first counts slots.
All inputs are finite; a program needn't handle non-finite values.
Results may differ from a plain program's by a relative error of at most 0.0017.
Values sent between devices are 32-bit elements; how exact they have to be, the bound alone decides.
A program may use at most 64 MiB of HBM per device.

v0:
```python
import jax
import jax.numpy as jnp
from jax import lax
from jax.sharding import PartitionSpec as P

STEPS = 8
PATCH = 8


def extended(x, sides, width):
    for axis, dim in sides:
        peers, length = (lax.axis_size(axis), x.shape[dim])
        up = [(i, (i + 1) % peers) for i in range(peers - 1)]
        down = [(j, i) for i, j in up]
        last = lax.slice_in_dim(x, length - width, length, axis=dim)
        first = lax.slice_in_dim(x, 0, width, axis=dim)
        before = lax.ppermute(last, axis, up)
        after = lax.ppermute(first, axis, down)
        x = jnp.concatenate([before, x, after], axis=dim)
    return x


def coefficient(material, speed_table):
    coef = jnp.zeros(material.shape, jnp.float32)
    for number in range(speed_table.shape[0]):
        coef = jnp.where(material == number, speed_table[number], coef)
    return coef


def update(prev, now, coef, padded):
    beside = padded[2:, 1:-1, 1:-1] + padded[:-2, 1:-1, 1:-1]
    beside = beside + padded[1:-1, 2:, 1:-1] + padded[1:-1, :-2, 1:-1]
    beside = beside + padded[1:-1, 1:-1, 2:] + padded[1:-1, 1:-1, :-2]
    return 2.0 * now - prev + coef * (beside - 6.0 * now)


def outer_sum(left, right):
    return lax.dot_general(
        left, right, (((0,), (0,)), ((), ())), preferred_element_type=jnp.float32
    )


def mlp_parts(inputs, targets, valid, total, w_in, w_out):
    scale = lax.rsqrt(jnp.mean(inputs * inputs, axis=-1, keepdims=True) + 1e-06)
    normed = (inputs * scale).astype(jnp.bfloat16)
    pre = jnp.dot(normed, w_in, preferred_element_type=jnp.float32)
    act = jax.nn.gelu(pre).astype(jnp.bfloat16)
    err = inputs + jnp.dot(act, w_out, preferred_element_type=jnp.float32) - targets
    dout = (2.0 * err * valid[:, None] / total).astype(jnp.bfloat16)
    dact = lax.dot_general(
        dout, w_out, (((1,), (1,)), ((), ())), preferred_element_type=jnp.float32
    )
    dpre = jax.vjp(jax.nn.gelu, pre)[1](dact)[0].astype(jnp.bfloat16)
    return (normed, act, dout, dpre)


def body(pressure_prev, pressure_now, material, speed_table, anchors, counts, w_in, w_out):
    coef = coefficient(material, speed_table)
    cells_x, cells_y, cells_z = pressure_now.shape
    prev, now = (pressure_prev, pressure_now)
    for step in range(STEPS):
        padded = extended(now, (("gx", 0), ("gy", 1), ("gz", 2)), 1)
        prev, now = (now, update(prev, now, coef, padded))
    local = anchors.reshape(-1)
    edge = jnp.arange(PATCH, dtype=jnp.int32)
    offsets = (
        edge[:, None, None] * (cells_y * cells_z)
        + edge[None, :, None] * cells_z
        + edge[None, None, :]
    ).reshape(-1)
    cell_index = local[:, None] + offsets[None, :]
    inputs = jnp.take(pressure_now.reshape(-1), cell_index, axis=0)
    targets = jnp.take(now.reshape(-1), cell_index, axis=0)
    slots = local.shape[0]
    used = counts.reshape(())
    total = lax.psum(used.astype(jnp.float32), ("gx", "gy", "gz"))
    valid = (jnp.arange(slots, dtype=jnp.int32) < used).astype(jnp.float32)
    normed, act, dout, dpre = mlp_parts(inputs, targets, valid, total, w_in, w_out)
    groups = lax.axis_size("gx")
    in_count = normed.shape[1] // groups
    out_count = act.shape[1] // groups
    full_in = outer_sum(normed, dpre)
    full_out = outer_sum(act, dout)
    summed_in, summed_out = lax.psum((full_in, full_out), ("gx", "gy", "gz"))
    position = lax.axis_index("gx")
    grad_in = lax.dynamic_slice_in_dim(summed_in, position * in_count, in_count, 0)
    grad_out = lax.dynamic_slice_in_dim(summed_out, position * out_count, out_count, 0)
    return (now, grad_in, grad_out)


def solution(mesh):
    return jax.shard_map(
        body,
        mesh=mesh,
        in_specs=(
            P("gx", "gy", "gz"),
            P("gx", "gy", "gz"),
            P("gx", "gy", "gz"),
            P(),
            P("gx", "gy", "gz"),
            P("gx", "gy", "gz"),
            P(),
            P(),
        ),
        out_specs=(P("gx", "gy", "gz"), P("gx", None), P("gx", None)),
        check_vma=False,
    )
```

profile of v0, /device:TPU:2, one launch (start us, length us, event | category | flops | bytes accessed | tf_op | source)
XLA Modules:
  0.0 1375.9 jit_solution(7897120378503387624)
XLA Ops:
  12.3 3.8 collective-permute-done
  17.4 4.5 collective-permute-start.3
  23.6 2.4 collective-permute-start.4
  26.1 3.4 collective-permute-start.5
  30.2 3.7 collective-permute-done.4
  33.9 2.7 collective-permute-done.5
  36.6 5.7 fusion.70
  43.6 3.6 collective-permute-start.7
  49.4 5.3 collective-permute-start.9
  58.4 3.9 collective-permute-start.11
  62.3 5.0 collective-permute-done.10
  67.3 1.9 collective-permute-done.11
  69.2 5.7 fusion.62
  76.2 3.3 collective-permute-start.13
  81.6 5.7 collective-permute-start.15
  91.0 4.0 collective-permute-start.17
  95.0 2.8 collective-permute-done.16
  99.6 5.7 fusion.54
  106.6 6.7 collective-permute-start.19
  115.5 5.4 collective-permute-start.21
  124.5 3.9 collective-permute-start.23
  128.4 2.8 collective-permute-done.22
  133.1 5.7 fusion.46
  140.1 7.6 collective-permute-start.25
  149.9 5.4 collective-permute-start.27
  158.9 3.9 collective-permute-start.29
  162.9 2.8 collective-permute-done.28
  167.6 5.7 fusion.38
  174.5 7.6 collective-permute-start.31
  184.3 5.4 collective-permute-start.33
  194.0 3.9 collective-permute-start.35
  198.1 2.8 collective-permute-done.34
  202.7 6.6 fusion.30
  210.6 7.3 collective-permute-start.37
  220.8 6.0 collective-permute-start.39
  227.1 362.7 %gather_fusion = f32[65536]{0:T(1024)S(1)} fusion(f32[98304]{0:T(1024)S(1)} %bitcast.25, s32[65536]{0:T(1024)S(1)} %broadcast_clamp_fusion), kind=kCustom, calls=%fused_computation.clone | custom fusion | bytes 786432 | tf_op jit(solution)/shard_map/jit(_take)/gather | solution.py:72
  590.9 2.1 collective-permute-start.40
  593.0 3.9 collective-permute-start.41
  597.1 2.5 collective-permute-done.40
  601.6 6.5 fusion.22
  609.4 7.9 collective-permute-start.43
  619.4 4.9 collective-permute-start.45
  629.1 4.1 collective-permute-start.47
  633.2 86.1 %psum.21 = f32[]{:T(128)} all-reduce(f32[]{:T(128)S(6)} %convert_element_type.22), channel_id=1, replica_groups=mesh['gx'=8,'gy'=8,'gz'=4] {'gx','gy','gz'}, use_global_device_ids=true, to_apply=%region_1.3 | all-reduce | flops 1 | bytes 8 | tf_op jit(solution)/shard_map/psum | solution.py:76
  720.0 6.7 fusion.14
  727.0 362.7 %gather_fusion.1 = f32[65536]{0:T(1024)S(1)} fusion(f32[98304]{0:T(1024)S(1)} %bitcast.24, s32[65536]{0:T(1024)S(1)} %broadcast_clamp_fusion), kind=kCustom, calls=%fused_computation.1.clone | custom fusion | bytes 786432 | tf_op jit(solution)/shard_map/jit(_take)/gather | solution.py:73
  1092.7 2.4 fusion.75
  1095.1 270.6 %all-reduce.3.cloned.1.call-done = (f32[512,1024]{1,0:T(8,128)}, f32[1024,512]{1,0:T(8,128)}) async-done(((f32[512,1024]{1,0:T(8,128)}, f32[1024,512]{1,0:T(8,128)}), (f32[512,1024]{1,0:T(8,128)}, f32[1024,512]{1,0:T(8,128)})) %all-reduce.3.cloned.1.call-update) | async-done | bytes 4194320 | tf_op jit(solution)/shard_map/psum | solution.py:84
  (146 shorter events, 74.5 us)
Async XLA Ops:
  7.2 1358.4 %all-reduce.3.cloned.1.call-start = ((), (), s32[]{:S(2)}) async-start(), calls=%async_computation | async-start | bytes 8388608 | tf_op jit(solution)/shard_map/psum | solution.py:84
  9.9 6.1 collective-permute-start
  16.1 5.9 collective-permute-start.2
  17.4 6.0 collective-permute-start.3
  23.6 10.2 collective-permute-start.4
  26.1 10.5 collective-permute-start.5
  42.3 4.9 collective-permute-start.6
  43.6 4.4 collective-permute-start.7
  48.1 6.7 collective-permute-start.8
  49.4 6.8 collective-permute-start.9
  56.4 10.9 collective-permute-start.10
  58.4 10.9 collective-permute-start.11
  74.9 4.6 collective-permute-start.12
  76.2 4.1 collective-permute-start.13
  80.3 7.0 collective-permute-start.14
  81.6 7.2 collective-permute-start.15
  89.1 8.7 collective-permute-start.16
  91.0 8.6 collective-permute-start.17
  105.3 8.0 collective-permute-start.18
  106.6 7.5 collective-permute-start.19
  114.2 6.7 collective-permute-start.20
  115.5 6.9 collective-permute-start.21
  122.6 8.6 collective-permute-start.22
  124.5 8.6 collective-permute-start.23
  138.8 8.9 collective-permute-start.24
  140.1 8.4 collective-permute-start.25
  148.6 6.7 collective-permute-start.26
  149.9 6.9 collective-permute-start.27
  157.0 8.6 collective-permute-start.28
  158.9 8.6 collective-permute-start.29
  173.2 8.9 collective-permute-start.30
  174.5 8.5 collective-permute-start.31
  183.0 6.8 collective-permute-start.32
  184.3 6.9 collective-permute-start.33
  192.1 8.8 collective-permute-start.34
  194.0 8.7 collective-permute-start.35
  209.3 8.8 collective-permute-start.36
  210.6 8.2 collective-permute-start.37
  219.5 370.4 %collective-permute-start.38 = (f32[18,1,256]{2,1,0:T(1,128)}, f32[18,1,256]{2,1,0:T(1,128)}, u32[]{:S(2)}, u32[]{:S(2)}) collective-permute-start(f32[18,1,256]{2,1,0:T(1,128)} %get-tuple-element.25), channel_id=1, source_target_pairs={{4,0},{8,4},{12,8},{16,12},{20,16},{24,20},{28,24},{5,1},{9,5},{13... | collective-permute-start | bytes 55304 | tf_op jit(solution)/shard_map/ppermute | solution.py:18
  220.8 369.1 %collective-permute-start.39 = (f32[18,1,256]{2,1,0:T(1,128)}, f32[18,1,256]{2,1,0:T(1,128)}, u32[]{:S(2)}, u32[]{:S(2)}) collective-permute-start(f32[18,1,256]{2,1,0:T(1,128)} %get-tuple-element.24), channel_id=1, source_target_pairs={{0,4},{4,8},{8,12},{12,16},{16,20},{20,24},{24,28},{1,5},{5,9},{9,... | collective-permute-start | bytes 55304 | tf_op jit(solution)/shard_map/ppermute | solution.py:17
  590.9 8.7 collective-permute-start.40
  593.0 8.6 collective-permute-start.41
  608.1 9.2 collective-permute-start.42
  609.4 8.8 collective-permute-start.43
  618.1 8.0 collective-permute-start.44
  619.4 6.7 collective-permute-start.45
  627.2 92.1 %collective-permute-start.46 = (f32[18,26,1]{2,1,0:T(8,128)}, f32[18,26,1]{2,1,0:T(8,128)S(1)}, u32[]{:S(2)}, u32[]{:S(2)}) collective-permute-start(f32[18,26,1]{2,1,0:T(8,128)} %get-tuple-element.6), channel_id=1, source_target_pairs={{1,0},{2,1},{3,2},{5,4},{6,5},{7,6},{9,8},{10,9},{11,10},{13,12},{... | collective-permute-start | bytes 5624 | tf_op jit(solution)/shard_map/ppermute | solution.py:18
  629.1 90.9 %collective-permute-start.47 = (f32[18,26,1]{2,1,0:T(8,128)}, f32[18,26,1]{2,1,0:T(8,128)}, u32[]{:S(2)}, u32[]{:S(2)}) collective-permute-start(f32[18,26,1]{2,1,0:T(8,128)} %get-tuple-element.7), channel_id=1, source_target_pairs={{0,1},{1,2},{2,3},{4,5},{5,6},{6,7},{8,9},{9,10},{10,11},{12,13},{... | collective-permute-start | bytes 5624 | tf_op jit(solution)/shard_map/ppermute | solution.py:17
  (15 other events, 2726.6 us)
Sparse Core Ops, SparseCore 0:
  1095.2 270.4 all-reduce.2
where the time goes:
time: 1380 us
  local copies, waits for them, and re-layouts  735 us (53%)
  waiting for transfers between devices  325 us (24%)
  starting transfers between devices  156 us (11%)
  blocking collectives  86.1 us (6%)
  other arithmetic  50.9 us (4%)
  between operations  15.7 us (1%)
    gather x2, local copies, waits for them, and re-layouts, body(): targets = jnp.take(now.reshape(-1), cell_index, axis=0)  363 us
    gather x2, local copies, waits for them, and re-layouts, body(): inputs = jnp.take(pressure_now.reshape(-1), cell_index, axis=0)  363 us
    psum x1, waiting for transfers between devices, body(): summed_in, summed_out = lax.psum((full_in, full_out), ('gx', 'gy', 'gz'))  271 us
    ppermute x24, starting transfers between devices, extended(): before = lax.ppermute(last, axis, up)  120 us
    psum x1, blocking collectives, body(): total = lax.psum(used.astype(jnp.float32), ('gx', 'gy', 'gz'))  86.1 us
    add x8, other arithmetic, update(): return 2.0 * now - prev + coef * (beside - 6.0 * now)  48.1 us
    ppermute x24, starting transfers between devices, extended(): after = lax.ppermute(first, axis, down)  36.7 us
    ppermute x24, waiting for transfers between devices, extended(): before = lax.ppermute(last, axis, up)  28.2 us
  transfers between devices with their start and end apart: 49, of which 29 were waited for; matrix products, arithmetic and copies ran while one was open for 27% of the time, Pallas kernels for 0%

commit v1 on v0

--- a/solution.py
+++ b/solution.py
@@ -81,7 +81,7 @@
     out_count = act.shape[1] // groups
     full_in = outer_sum(normed, dpre)
     full_out = outer_sum(act, dout)
-    summed_in, summed_out = lax.psum((full_in, full_out), ("gx", "gy", "gz"))
+    summed_in, summed_out = lax.psum(lax.psum((full_in, full_out), ("gy", "gz")), "gx")
     position = lax.axis_index("gx")
     grad_in = lax.dynamic_slice_in_dim(summed_in, position * in_count, in_count, 0)
     grad_out = lax.dynamic_slice_in_dim(summed_out, position * out_count, out_count, 0)

time: 1380 us -> 1550 us (1.12)
  waiting for transfers between devices: 325 us -> 500 us
    psum x1 -> x2, waiting for transfers between devices: 271 us -> 445 us  [the longest x1 326 us: body(): lax.psum((full_in, full_out), ('gy', 'gz'))]
  transfers between devices with their start and end apart: 49 -> 50, of which waited for: 29 -> 30; matrix products, arithmetic and copies ran while one was open for 27% -> 24% of each run, Pallas kernels for 0% -> 0%
where the time goes in v1:
time: 1550 us
  local copies, waits for them, and re-layouts  735 us (47%)
  waiting for transfers between devices  500 us (32%)
  starting transfers between devices  156 us (10%)
  blocking collectives  86.1 us (6%)
  other arithmetic  49.8 us (3%)
  between operations  15.7 us (1%)
    gather x2, local copies, waits for them, and re-layouts, body(): inputs = jnp.take(pressure_now.reshape(-1), cell_index, axis=0)  363 us
    gather x2, local copies, waits for them, and re-layouts, body(): targets = jnp.take(now.reshape(-1), cell_index, axis=0)  363 us
    psum x1, waiting for transfers between devices, body(): lax.psum((full_in, full_out), ('gy', 'gz'))  326 us
    ppermute x24, starting transfers between devices, extended(): before = lax.ppermute(last, axis, up)  120 us
    psum x1, waiting for transfers between devices, body(): lax.psum(lax.psum((full_in, full_out), ('gy', 'gz')), 'gx')  119 us
    psum x1, blocking collectives, body(): total = lax.psum(used.astype(jnp.float32), ('gx', 'gy', 'gz'))  86.1 us
    add x8, other arithmetic, update(): return 2.0 * now - prev + coef * (beside - 6.0 * now)  47 us
    ppermute x24, starting transfers between devices, extended(): after = lax.ppermute(first, axis, down)  36.7 us
  transfers between devices with their start and end apart: 50, of which 30 were waited for; matrix products, arithmetic and copies ran while one was open for 24% of the time, Pallas kernels for 0%

profile of v1, /device:TPU:2, one launch (start us, length us, event | category | flops | bytes accessed | tf_op | source)
XLA Modules:
  0.0 1549.5 jit_solution(15967348472203398156)
XLA Ops:
  12.3 3.8 collective-permute-done
  17.4 4.5 collective-permute-start.3
  23.6 2.4 collective-permute-start.4
  26.1 3.4 collective-permute-start.5
  30.2 3.7 collective-permute-done.4
  33.9 2.7 collective-permute-done.5
  36.6 5.5 fusion.70
  43.5 3.6 collective-permute-start.7
  49.2 5.3 collective-permute-start.9
  58.2 3.9 collective-permute-start.11
  62.2 5.0 collective-permute-done.10
  69.1 5.5 fusion.62
  75.9 3.3 collective-permute-start.13
  81.4 5.7 collective-permute-start.15
  90.7 4.0 collective-permute-start.17
  94.7 2.8 collective-permute-done.16
  99.4 5.5 fusion.54
  106.2 6.7 collective-permute-start.19
  115.1 5.4 collective-permute-start.21
  124.1 3.9 collective-permute-start.23
  128.1 2.8 collective-permute-done.22
  132.7 5.5 fusion.46
  139.6 7.6 collective-permute-start.25
  149.4 5.4 collective-permute-start.27
  158.4 3.9 collective-permute-start.29
  162.4 2.8 collective-permute-done.28
  167.0 5.5 fusion.38
  173.9 7.6 collective-permute-start.31
  183.7 5.4 collective-permute-start.33
  193.4 3.9 collective-permute-start.35
  197.5 2.8 collective-permute-done.34
  202.1 6.5 fusion.30
  209.9 7.3 collective-permute-start.37
  220.0 6.0 collective-permute-start.39
  226.3 362.7 %gather_fusion = f32[65536]{0:T(1024)S(1)} fusion(f32[98304]{0:T(1024)S(1)} %bitcast.25, s32[65536]{0:T(1024)S(1)} %broadcast_clamp_fusion), kind=kCustom, calls=%fused_computation.clone | custom fusion | bytes 786432 | tf_op jit(solution)/shard_map/jit(_take)/gather | solution.py:72
  590.1 2.1 collective-permute-start.40
  592.2 3.9 collective-permute-start.41
  596.3 2.5 collective-permute-done.40
  600.8 6.3 fusion.22
  608.5 7.9 collective-permute-start.43
  618.5 4.8 collective-permute-start.45
  628.2 4.1 collective-permute-start.47
  632.3 86.1 %psum.35 = f32[]{:T(128)} all-reduce(f32[]{:T(128)S(6)} %convert_element_type.22), channel_id=1, replica_groups=mesh['gx'=8,'gy'=8,'gz'=4] {'gx','gy','gz'}, use_global_device_ids=true, to_apply=%region_1.3 | all-reduce | flops 1 | bytes 8 | tf_op jit(solution)/shard_map/psum | solution.py:76
  719.1 6.5 fusion.14
  725.9 362.7 %gather_fusion.1 = f32[65536]{0:T(1024)S(1)} fusion(f32[98304]{0:T(1024)S(1)} %bitcast.24, s32[65536]{0:T(1024)S(1)} %broadcast_clamp_fusion), kind=kCustom, calls=%fused_computation.1.clone | custom fusion | bytes 786432 | tf_op jit(solution)/shard_map/jit(_take)/gather | solution.py:73
  1091.6 2.4 fusion.75
  1094.1 326.0 %all-reduce.5.cloned.1.call-done = (f32[512,1024]{1,0:T(8,128)}, f32[1024,512]{1,0:T(8,128)}) async-done(((f32[512,1024]{1,0:T(8,128)}, f32[1024,512]{1,0:T(8,128)}), (f32[512,1024]{1,0:T(8,128)}, f32[1024,512]{1,0:T(8,128)})) %all-reduce.5.cloned.1.call-update) | async-done | bytes 4194320 | tf_op jit(solution)/shard_map/psum | solution.py:84
  1420.1 119.2 %all-reduce.7.cloned.1.call-done = (f32[512,1024]{1,0:T(8,128)}, f32[1024,512]{1,0:T(8,128)}) async-done(((f32[512,1024]{1,0:T(8,128)}, f32[1024,512]{1,0:T(8,128)}), (f32[512,1024]{1,0:T(8,128)}, f32[1024,512]{1,0:T(8,128)})) %all-reduce.7.cloned.1.call-update) | async-done | bytes 4194320 | tf_op jit(solution)/shard_map/psum | solution.py:84
  (149 shorter events, 76.4 us)
Async XLA Ops:
  7.2 1412.8 %all-reduce.5.cloned.1.call-start = ((), (), s32[]{:S(2)}) async-start(), calls=%async_computation | async-start | bytes 8388608 | tf_op jit(solution)/shard_map/psum | solution.py:84
  9.9 6.1 collective-permute-start
  16.1 5.9 collective-permute-start.2
  17.4 6.0 collective-permute-start.3
  23.6 10.2 collective-permute-start.4
  26.1 10.5 collective-permute-start.5
  42.2 4.9 collective-permute-start.6
  43.5 4.4 collective-permute-start.7
  47.9 6.7 collective-permute-start.8
  49.2 6.8 collective-permute-start.9
  56.3 10.9 collective-permute-start.10
  58.2 10.9 collective-permute-start.11
  74.6 4.6 collective-permute-start.12
  80.1 7.0 collective-permute-start.14
  81.4 7.2 collective-permute-start.15
  88.8 8.7 collective-permute-start.16
  90.7 8.6 collective-permute-start.17
  104.9 8.0 collective-permute-start.18
  106.2 7.5 collective-permute-start.19
  113.8 6.7 collective-permute-start.20
  115.1 6.9 collective-permute-start.21
  122.2 8.6 collective-permute-start.22
  124.1 8.6 collective-permute-start.23
  138.3 8.9 collective-permute-start.24
  139.6 8.4 collective-permute-start.25
  148.1 6.7 collective-permute-start.26
  149.4 6.9 collective-permute-start.27
  156.5 8.6 collective-permute-start.28
  158.4 8.6 collective-permute-start.29
  172.6 8.9 collective-permute-start.30
  173.9 8.5 collective-permute-start.31
  182.4 6.8 collective-permute-start.32
  183.7 6.9 collective-permute-start.33
  191.4 8.8 collective-permute-start.34
  193.4 8.7 collective-permute-start.35
  208.6 8.8 collective-permute-start.36
  209.9 8.2 collective-permute-start.37
  218.7 370.4 %collective-permute-start.38 = (f32[18,1,256]{2,1,0:T(1,128)}, f32[18,1,256]{2,1,0:T(1,128)}, u32[]{:S(2)}, u32[]{:S(2)}) collective-permute-start(f32[18,1,256]{2,1,0:T(1,128)} %get-tuple-element.27), channel_id=1, source_target_pairs={{4,0},{8,4},{12,8},{16,12},{20,16},{24,20},{28,24},{5,1},{9,5},{13... | collective-permute-start | bytes 55304 | tf_op jit(solution)/shard_map/ppermute | solution.py:18
  220.0 369.1 %collective-permute-start.39 = (f32[18,1,256]{2,1,0:T(1,128)}, f32[18,1,256]{2,1,0:T(1,128)}, u32[]{:S(2)}, u32[]{:S(2)}) collective-permute-start(f32[18,1,256]{2,1,0:T(1,128)} %get-tuple-element.26), channel_id=1, source_target_pairs={{0,4},{4,8},{8,12},{12,16},{16,20},{20,24},{24,28},{1,5},{5,9},{9,... | collective-permute-start | bytes 55304 | tf_op jit(solution)/shard_map/ppermute | solution.py:17
  590.1 8.7 collective-permute-start.40
  592.2 8.6 collective-permute-start.41
  607.2 9.2 collective-permute-start.42
  608.5 8.8 collective-permute-start.43
  617.2 8.0 collective-permute-start.44
  618.5 6.7 collective-permute-start.45
  626.3 92.1 %collective-permute-start.46 = (f32[18,26,1]{2,1,0:T(8,128)}, f32[18,26,1]{2,1,0:T(8,128)S(1)}, u32[]{:S(2)}, u32[]{:S(2)}) collective-permute-start(f32[18,26,1]{2,1,0:T(8,128)} %get-tuple-element.8), channel_id=1, source_target_pairs={{1,0},{2,1},{3,2},{5,4},{6,5},{7,6},{9,8},{10,9},{11,10},{13,12},{... | collective-permute-start | bytes 5624 | tf_op jit(solution)/shard_map/ppermute | solution.py:18
  628.2 91.0 %collective-permute-start.47 = (f32[18,26,1]{2,1,0:T(8,128)}, f32[18,26,1]{2,1,0:T(8,128)}, u32[]{:S(2)}, u32[]{:S(2)}) collective-permute-start(f32[18,26,1]{2,1,0:T(8,128)} %get-tuple-element.9), channel_id=1, source_target_pairs={{0,1},{1,2},{2,3},{4,5},{5,6},{6,7},{8,9},{9,10},{10,11},{12,13},{... | collective-permute-start | bytes 5624 | tf_op jit(solution)/shard_map/ppermute | solution.py:17
  1094.0 445.3 %all-reduce.7.cloned.1.call-start = ((), (), s32[]{:S(2)}) async-start(), calls=%async_computation.1 | async-start | bytes 8388608 | tf_op jit(solution)/shard_map/psum | solution.py:84
  (16 other events, 2729.4 us)
Sparse Core Ops, SparseCore 0:
  1094.1 325.8 all-reduce.4
  1422.8 116.5 all-reduce.6
